TPU v7x, 256 devices: a whole 4x4x8 slice. The times are simulated.
256 devices in a mesh: req: 16 (over z_hi, x), mp: 16 (over z_lo, y, core).
Axes of the slice: x: 4, y: 4, z: 8 (z_hi: 4, z_lo: 2; z = z_hi * 2 + z_lo), core: 2. Of those that a mesh axis runs over, the one named last changes fastest.
Arguments:
- queries: bfloat16 [2048, 4096], P('req', 'mp'), may hold values from -6 to 6
- suffix_kv: bfloat16 [2, 2048, 4096], P(None, 'req', 'mp'), may hold values from -6 to 6
- prefix_kv: bfloat16 [2, 8192, 4096], P(None, 'req', 'mp'), may hold values from -6 to 6
- resid: bfloat16 [2048, 4096], P('req', 'mp'), may hold values from -6 to 6
- ln_gain: float32 [4096], replicated, may hold values from 0.1 to 1.9
- out_weight: bfloat16 [4096, 4096], P('mp'), may hold values from -0.125 to 0.125
- up_weight: bfloat16 [4096, 8192], P(None, 'mp'), may hold values from -0.09375 to 0.09375
- down_weight: bfloat16 [8192, 4096], P('mp'), may hold values from -0.09375 to 0.09375
- lengths: int32 [16], replicated, may hold values from 1 to 128, 1024 in all
- req_group: int32 [16], replicated, may hold values from 0 to 3, as said below
- prefix_owner: int32 [16], replicated, may hold values from 0 to 15, as said below
Outputs:
- attended: bfloat16 [2048, 4096], P('req', 'mp')
- layer_out: bfloat16 [2048, 4096], P('req', 'mp')
Inputs may be any that keep to these rules, and one draw needn't show every extreme that they name: `req_group`: each of the 4 groups holds exactly 4 requests. `prefix_owner`: a permutation: every logical block is held by exactly one stored block.
All inputs are finite; a program needn't handle non-finite values.
Results may differ from a plain program's by a relative error of at most 0.029.
Values may be sent and summed in bfloat16 or wider, within the bound.
A program may use at most 128 MiB of HBM per device.

v0:
```python
import jax
import jax.numpy as jnp
from jax import lax
from jax.sharding import PartitionSpec as P

H = 32
DH = 128
KB = 512
S_MAX = 128
P_SIZE = 2048
very_negative = -1e30


def block_partial(query_rows, key_rows, value_rows, query_pos, key_pos, allowed, slopes, shared):
    if shared:
        score_form = "rqhd,khd->rqhk"
        value_form = "rqhk,khd->rqhd"
    else:
        score_form = "rqhd,rkhd->rqhk"
        value_form = "rqhk,rkhd->rqhd"
    scores = jnp.einsum(
        score_form, query_rows, key_rows, preferred_element_type=jnp.float32
    ) * float(DH) ** (-0.5)
    distance = (query_pos[:, None, None] - key_pos[None, None, :]).astype(jnp.float32)
    scores = scores - slopes[None, :, None] * distance
    masked = jnp.where(allowed, scores, very_negative)
    maxima = jnp.max(masked, axis=-1)
    weights = jnp.where(allowed, jnp.exp(masked - maxima[..., None]), 0.0)
    totals = jnp.sum(weights, axis=-1)
    rounded = weights.astype(jnp.bfloat16)
    weighted = jnp.einsum(value_form, rounded, value_rows, preferred_element_type=jnp.float32)
    return (weighted, maxima, totals)


def combine(first_part, second_part):
    peak_max = jnp.maximum(first_part[1], second_part[1])
    scale_first = jnp.exp(first_part[1] - peak_max)
    scale_second = jnp.exp(second_part[1] - peak_max)
    weighted = first_part[0] * scale_first[..., None] + second_part[0] * scale_second[..., None]
    return (weighted, peak_max, first_part[2] * scale_first + second_part[2] * scale_second)


def shards(
    queries,
    suffix_kv,
    prefix_kv,
    resid,
    ln_gain,
    out_weight,
    up_weight,
    down_weight,
    lengths,
    req_group,
    prefix_owner,
):
    row_count = queries.shape[0]
    local_req = row_count // S_MAX
    columns = queries.shape[1]
    head_count = columns // DH
    per_group = P_SIZE // KB
    first_req = lax.axis_index("req") * local_req
    col_start = lax.axis_index("mp") * columns
    my_len = lax.dynamic_slice_in_dim(lengths, first_req, local_req)
    my_group = lax.dynamic_slice_in_dim(req_group, first_req, local_req)
    head_ids = (lax.axis_index("mp") * head_count + jnp.arange(head_count)).astype(jnp.float32)
    slopes = jnp.power(2.0, -8.0 * (head_ids + 1.0) / H)
    my_query = queries.reshape(local_req, S_MAX, head_count, DH)
    suffix_local = suffix_kv.reshape(2, local_req, S_MAX, head_count, DH)
    offsets = jnp.arange(S_MAX)
    query_pos = P_SIZE + offsets
    allowed = (offsets[None, None, :] <= offsets[None, :, None]) & (
        offsets[None, None, :] < my_len[:, None, None]
    )
    own_part = block_partial(
        my_query,
        suffix_local[0],
        suffix_local[1],
        query_pos,
        query_pos,
        allowed[:, :, None, :],
        slopes,
        False,
    )
    key_offsets = jnp.arange(KB)
    shard_piece = lax.all_gather(prefix_kv, "req", axis=1, tiled=True)
    block_total = shard_piece.shape[1] // KB
    blocks_here = shard_piece.reshape(2, block_total, KB, head_count, DH)

    def fold_step(block_index, inner_state):
        logical = prefix_owner[block_index]
        same_group = my_group == logical // per_group
        base_pos = logical % per_group * KB

        def attend_block(state_in):
            fresh = block_partial(
                my_query,
                blocks_here[0, block_index],
                blocks_here[1, block_index],
                query_pos,
                base_pos + key_offsets,
                same_group[:, None, None, None],
                slopes,
                True,
            )
            return combine(state_in, fresh)

        return lax.cond(jnp.any(same_group), attend_block, lambda state_in: state_in, inner_state)

    result = lax.fori_loop(0, block_total, fold_step, own_part)
    outcome = result[0] / result[2][..., None]
    live_mask = offsets[None, :] < my_len[:, None]
    attended = (
        jnp.where(live_mask[:, :, None, None], outcome, 0.0)
        .astype(jnp.bfloat16)
        .reshape(row_count, columns)
    )
    head_term = jnp.dot(attended, out_weight, preferred_element_type=jnp.float32)
    own_columns = lax.dynamic_slice_in_dim(head_term, col_start, columns, 1) + resid.astype(
        jnp.float32
    )
    head_term = lax.dynamic_update_slice_in_dim(head_term, own_columns, col_start, 1)
    mixed_rows = lax.psum(head_term.astype(jnp.bfloat16), "mp").astype(jnp.float32)
    row_mean = jnp.mean(mixed_rows, axis=1, keepdims=True)
    centered = mixed_rows - row_mean
    variance = jnp.mean(centered * centered, axis=1, keepdims=True)
    normed = (centered * lax.rsqrt(variance + 1e-05) * ln_gain).astype(jnp.bfloat16)
    hidden = jax.nn.gelu(
        jnp.dot(normed, up_weight, preferred_element_type=jnp.float32), approximate=False
    ).astype(jnp.bfloat16)
    projected = jnp.dot(hidden, down_weight, preferred_element_type=jnp.float32)
    update = lax.psum_scatter(
        projected.astype(jnp.bfloat16), "mp", scatter_dimension=1, tiled=True
    ).astype(jnp.float32)
    mixed_own = lax.dynamic_slice_in_dim(mixed_rows, col_start, columns, 1)
    layer_out = jnp.where(live_mask.reshape(row_count)[:, None], mixed_own + update, 0.0).astype(
        jnp.bfloat16
    )
    return (attended, layer_out)


def solution(mesh):
    placed = (
        P("req", "mp"),
        P(None, "req", "mp"),
        P(None, "req", "mp"),
        P("req", "mp"),
        P(),
        P("mp", None),
        P(None, "mp"),
        P("mp", None),
        P(),
        P(),
        P(),
    )
    return jax.shard_map(
        shards,
        mesh=mesh,
        in_specs=placed,
        out_specs=(P("req", "mp"), P("req", "mp")),
        check_vma=False,
    )
```

profile of v0, /device:TPU:6, one launch (start us, length us, event | category | flops | bytes accessed | tf_op | source)
XLA Modules:
  0.0 440.7 jit_solution(7493433449119299911)
XLA Ops:
  8.0 1.2 dynamic_slice.35
  9.2 1.2 dynamic_slice.34
  14.9 107.0 %all-gather.2.cloned.1.call-done = bf16[2,8192,256]{2,1,0:T(8,128)(2,1)} async-done(((bf16[2,512,256]{2,1,0:T(8,128)(2,1)}), bf16[2,8192,256]{2,1,0:T(8,128)(2,1)}) %all-gather.2.cloned.1.call-update) | async-done | bytes 8388624 | tf_op jit(solution)/shard_map/all_gather | solution.py:85
  121.9 12.5 %reshape.277 = bf16[2,16,512,2,128]{4,3,2,1,0:T(2,128)(2,1)} reshape(bf16[2,8192,256]{2,1,0:T(8,128)(2,1)} %all-gather.2.cloned.1.call-done) | data formatting | bytes 16777216 | tf_op jit(solution)/shard_map/reshape | solution.py:87
  134.4 8.8 %copy.30 = bf16[2,16,512,2,128]{4,2,3,1,0:T(8,128)(2,1)} copy(bf16[2,16,512,2,128]{4,3,2,1,0:T(2,128)(2,1)} %reshape.277) | data formatting | bytes 16777216
  143.2 79.0 %while.20 = (s32[]{:T(128)}, f32[1,128,2,128]{1,3,2,0:T(8,128)S(1)}, f32[1,128,2]{1,2,0:T(2,128)S(1)}, f32[1,128,2]{1,2,0:T(2,128)S(1)}, s32[16]{0:T(128)S(1)}, ...) while((s32[]{:T(128)}, ...), condition=%wide.region_7.8_spmd.clone, body=%wide.region_2.7_spmd.clone.sunk | while | flops 68782248 | bytes 2980505 | solution.py:109
  150.7 4.7 %conditional.3 = ((f32[1,128,2,128]{1,3,2,0:T(8,128)S(1)}, f32[1,128,2]{1,2,0:T(2,128)S(1)}, f32[1,128,2]{1,2,0:T(2,128)S(1)})) conditional(s32[]{:T(128)} %bitcast.111, (f32[1,128,2,128]{1,3,2,0:T(8,128)S(1)}, f32[1,128,2]{1,2,0:T(2,128)S(1)}, f32[1,128,2]{1,2,0:T(2,128)S(1)}) %tuple.96, (pred[1]{0:T(512)(128)(4,1)}, s32[]{:T(128)}, ...), branch_computations={%region_3.3_spmd, %region_4.6_spmd.clone} | conditional | flops 68782224 | bytes 2977504 | solution.py:107
  154.1 1.3 fusion.10
  174.2 4.7 %conditional.3 = ((f32[1,128,2,128]{1,3,2,0:T(8,128)S(1)}, f32[1,128,2]{1,2,0:T(2,128)S(1)}, f32[1,128,2]{1,2,0:T(2,128)S(1)})) conditional(s32[]{:T(128)} %bitcast.111, (f32[1,128,2,128]{1,3,2,0:T(8,128)S(1)}, f32[1,128,2]{1,2,0:T(2,128)S(1)}, f32[1,128,2]{1,2,0:T(2,128)S(1)}) %tuple.96, (pred[1]{0:T(512)(128)(4,1)}, s32[]{:T(128)}, ...), branch_computations={%region_3.3_spmd, %region_4.6_spmd.clone} | conditional | flops 68782224 | bytes 2977504 | solution.py:107
  176.3 1.2 fusion.120
  177.7 1.3 fusion.10
  190.2 4.7 %conditional.3 = ((f32[1,128,2,128]{1,3,2,0:T(8,128)S(1)}, f32[1,128,2]{1,2,0:T(2,128)S(1)}, f32[1,128,2]{1,2,0:T(2,128)S(1)})) conditional(s32[]{:T(128)} %bitcast.111, (f32[1,128,2,128]{1,3,2,0:T(8,128)S(1)}, f32[1,128,2]{1,2,0:T(2,128)S(1)}, f32[1,128,2]{1,2,0:T(2,128)S(1)}) %tuple.96, (pred[1]{0:T(512)(128)(4,1)}, s32[]{:T(128)}, ...), branch_computations={%region_3.3_spmd, %region_4.6_spmd.clone} | conditional | flops 68782224 | bytes 2977504 | solution.py:107
  192.3 1.2 fusion.120
  193.6 1.3 fusion.10
  217.5 4.7 %conditional.3 = ((f32[1,128,2,128]{1,3,2,0:T(8,128)S(1)}, f32[1,128,2]{1,2,0:T(2,128)S(1)}, f32[1,128,2]{1,2,0:T(2,128)S(1)})) conditional(s32[]{:T(128)} %bitcast.111, (f32[1,128,2,128]{1,3,2,0:T(8,128)S(1)}, f32[1,128,2]{1,2,0:T(2,128)S(1)}, f32[1,128,2]{1,2,0:T(2,128)S(1)}) %tuple.96, (pred[1]{0:T(512)(128)(4,1)}, s32[]{:T(128)}, ...), branch_computations={%region_3.3_spmd, %region_4.6_spmd.clone} | conditional | flops 68782224 | bytes 2977504 | solution.py:107
  219.5 1.2 fusion.120
  220.9 1.3 fusion.10
  224.3 132.2 %all-reduce.2.cloned.1.call-done = bf16[128,4096]{1,0:T(8,128)(2,1)} async-done(((bf16[128,4096]{1,0:T(8,128)(2,1)}), bf16[128,4096]{1,0:T(8,128)(2,1)}) %all-reduce.2.cloned.1.call-update) | async-done | bytes 1048592 | tf_op jit(solution)/shard_map/psum | solution.py:122
  356.5 1.5 convert_reduce_fusion
  358.1 1.7 multiply_reduce_fusion
  359.8 6.4 %convolution_convert_fusion = bf16[128,4096]{1,0:T(8,128)(2,1)} fusion(bf16[512,4096]{1,0:T(8,128)(2,1)} %param.22, bf16[4096,512]{1,0:T(8,128)(2,1)} %param.21, bf16[128,4096]{1,0:T(8,128)(2,1)S(1)} %copy-done.1, f32[4096]{0:T(1024)S(1)} %copy-done.3, f32[128]{0:T(128)S(1)} %add_rsqrt_fusion, f32[128]{0:T(128)S(1)} %broadcast_multiply_fusion), kind=kOutput, calls=%fused_computation.40 | convolution fusion | flops 1081147392 | bytes 10503168 | tf_op jit(solution)/shard_map/dot_general | solution.py:130
  367.0 1.6 convert_element_type.81
  368.5 63.9 %reduce-scatter.2.cloned.1.call-done = bf16[128,256]{1,0:T(8,128)(2,1)} async-done(((bf16[128,4096]{1,0:T(8,128)(2,1)}), bf16[128,256]{1,0:T(8,128)(2,1)}) %reduce-scatter.2.cloned.1.call-update) | async-done | bytes 65552 | tf_op jit(solution)/shard_map/reduce_scatter | solution.py:131
  432.5 1.7 select_convert_fusion
  (146 shorter events, 20.4 us)
Async XLA Ops:
  7.2 215.1 %copy-start = (bf16[256,4096]{1,0:T(8,128)(2,1)S(1)}, bf16[256,4096]{1,0:T(8,128)(2,1)}, u32[]{:S(2)}) copy-start(bf16[256,4096]{1,0:T(8,128)(2,1)} %param.20) | copy-start | bytes 6291460
  7.2 114.7 %all-gather.2.cloned.1.call-start = ((), (), s32[]{:S(2)}) async-start(), calls=%async_computation.1 | async-start | bytes 8912896 | tf_op jit(solution)/shard_map/all_gather | solution.py:85
  7.9 348.6 %all-reduce.2.cloned.1.call-start = ((), (), s32[]{:S(2)}) async-start(), calls=%async_computation.2 | async-start | bytes 2097152 | tf_op jit(solution)/shard_map/psum | solution.py:122
  134.4 8.8 %copy-start.4 = (s32[16]{0:T(128)S(1)}, s32[16]{0:T(128)}, u32[]{:S(2)}) copy-start(s32[16]{0:T(128)} %param.25) | copy-start | bytes 196
  222.2 0.8 copy-start.2
  224.3 135.5 %copy-start.3 = (f32[4096]{0:T(1024)S(1)}, f32[4096]{0:T(1024)}, u32[]{:S(2)}) copy-start(f32[4096]{0:T(1024)} %param.19) | copy-start | bytes 49156
  224.3 208.2 %reduce-scatter.2.cloned.1.call-start = ((), (), s32[]{:S(2)}) async-start(), calls=%async_computation.3 | async-start | bytes 1114112 | tf_op jit(solution)/shard_map/reduce_scatter | solution.py:131
  356.5 3.2 copy-start.1
Sparse Core Ops, SparseCore 0:
  10.4 111.4 all-gather.1
  224.4 132.0 all-reduce.1
  366.3 66.0 reduce-scatter.1
where the time goes:
time: 442 us; the launch traced here: 441 us
  waiting for transfers between devices  304 us (69%)
  loops' own time  58.2 us (13%)
  local copies, waits for them, and re-layouts  36.9 us (8%)
  matrix products  18.1 us (4%)
  between operations  13.9 us (3%)
  other arithmetic  9.68 us (2%)
    psum x1, waiting for transfers between devices, shards(): lax.psum(head_term.astype(jnp.bfloat16), 'mp').astype(jnp.float32)  132 us
    all_gather x1, waiting for transfers between devices, shards(): shard_piece = lax.all_gather(prefix_kv, 'req', axis=1, tiled=True)  107 us
    reduce_scatter x1, waiting for transfers between devices, shards(): lax.psum_scatter(projected.astype(jnp.bfloat16), 'mp', scatter_dimension=...  63.9 us
    another operation x1, loops' own time, shards(): result = lax.fori_loop(0, block_total, fold_step, own_part)  50.1 us
    reshape x1, local copies, waits for them, and re-layouts, shards(): blocks_here = shard_piece.reshape(2, block_total, KB, head_count, DH)  12.5 us
    unnamed x17, local copies, waits for them, and re-layouts  11.3 us
    dynamic_slice x16, local copies, waits for them, and re-layouts, fold_step(): logical = prefix_owner[block_index]  9.59 us
  transfers between devices with their start and end apart: 3, of which 3 were waited for; matrix products, arithmetic and copies ran while one was open for 2% of the time, Pallas kernels for 0%

commit v1 on v0

--- a/solution.py
+++ b/solution.py
@@ -119,7 +119,9 @@
         jnp.float32
     )
     head_term = lax.dynamic_update_slice_in_dim(head_term, own_columns, col_start, 1)
-    mixed_rows = lax.psum(head_term.astype(jnp.bfloat16), "mp").astype(jnp.float32)
+    mixed_rows = jnp.sum(lax.all_gather(head_term.astype(jnp.bfloat16), "mp"), axis=0).astype(
+        jnp.float32
+    )
     row_mean = jnp.mean(mixed_rows, axis=1, keepdims=True)
     centered = mixed_rows - row_mean
     variance = jnp.mean(centered * centered, axis=1, keepdims=True)

time: 442 us -> 418 us (0.946)
  waiting for transfers between devices: 304 us -> 273 us
  other arithmetic: 9.68 us -> 16 us
    psum x1 -> x0, waiting for transfers between devices: 132 us -> none  [shards(): lax.psum(head_term.astype(jnp.bfloat16), 'mp').astype(jnp.float32)]
    all_gather x0 -> x1, waiting for transfers between devices: none -> 101 us  [shards(): lax.all_gather(head_term.astype(jnp.bfloat16), 'mp')]
    reduce_sum x0 -> x1, other arithmetic: none -> 8.93 us  [shards(): jnp.sum(lax.all_gather(head_term.astype(jnp.bfloat16), 'mp'), axis=0)]
    unnamed x17 -> x15, local copies, waits for them, and re-layouts: 11.3 us -> 11.4 us
where the time goes in v1:
time: 418 us; the launch traced here: 416 us
  waiting for transfers between devices  273 us (65%)
  loops' own time  58.2 us (14%)
  local copies, waits for them, and re-layouts  36.9 us (9%)
  matrix products  18.1 us (4%)
  other arithmetic  16 us (4%)
  between operations  13.9 us (3%)
    all_gather x1, waiting for transfers between devices, shards(): shard_piece = lax.all_gather(prefix_kv, 'req', axis=1, tiled=True)  107 us
    all_gather x1, waiting for transfers between devices, shards(): lax.all_gather(head_term.astype(jnp.bfloat16), 'mp')  101 us
    reduce_scatter x1, waiting for transfers between devices, shards(): lax.psum_scatter(projected.astype(jnp.bfloat16), 'mp', scatter_dimension=...  63.6 us
    another operation x1, loops' own time, shards(): result = lax.fori_loop(0, block_total, fold_step, own_part)  50.1 us
    reshape x1, local copies, waits for them, and re-layouts, shards(): blocks_here = shard_piece.reshape(2, block_total, KB, head_count, DH)  12.5 us
    unnamed x15, local copies, waits for them, and re-layouts  11.4 us
    dynamic_slice x16, local copies, waits for them, and re-layouts, fold_step(): logical = prefix_owner[block_index]  9.59 us
    reduce_sum x1, other arithmetic, shards(): jnp.sum(lax.all_gather(head_term.astype(jnp.bfloat16), 'mp'), axis=0)  8.93 us
  transfers between devices with their start and end apart: 3, of which 3 were waited for; matrix products, arithmetic and copies ran while one was open for 2% of the time, Pallas kernels for 0%

profile of v1, /device:TPU:6, one launch (start us, length us, event | category | flops | bytes accessed | tf_op | source)
XLA Modules:
  0.0 415.9 jit_solution(7991976849089987524)
XLA Ops:
  8.0 1.2 dynamic_slice.35
  9.2 1.2 dynamic_slice.34
  14.9 107.0 %all-gather.4.cloned.1.call-done = bf16[2,8192,256]{2,1,0:T(8,128)(2,1)} async-done(((bf16[2,512,256]{2,1,0:T(8,128)(2,1)}), bf16[2,8192,256]{2,1,0:T(8,128)(2,1)}) %all-gather.4.cloned.1.call-update) | async-done | bytes 8388624 | tf_op jit(solution)/shard_map/all_gather | solution.py:85
  121.9 12.5 %reshape.278 = bf16[2,16,512,2,128]{4,3,2,1,0:T(2,128)(2,1)} reshape(bf16[2,8192,256]{2,1,0:T(8,128)(2,1)} %all-gather.4.cloned.1.call-done) | data formatting | bytes 16777216 | tf_op jit(solution)/shard_map/reshape | solution.py:87
  134.4 8.8 %copy.30 = bf16[2,16,512,2,128]{4,2,3,1,0:T(8,128)(2,1)} copy(bf16[2,16,512,2,128]{4,3,2,1,0:T(2,128)(2,1)} %reshape.278) | data formatting | bytes 16777216
  143.2 79.0 %while.20 = (s32[]{:T(128)}, f32[1,128,2,128]{1,3,2,0:T(8,128)S(1)}, f32[1,128,2]{1,2,0:T(2,128)S(1)}, f32[1,128,2]{1,2,0:T(2,128)S(1)}, s32[16]{0:T(128)S(1)}, ...) while((s32[]{:T(128)}, ...), condition=%wide.region_7.8_spmd.clone, body=%wide.region_2.7_spmd.clone.sunk | while | flops 68782248 | bytes 2980505 | solution.py:109
  150.7 4.7 %conditional.3 = ((f32[1,128,2,128]{1,3,2,0:T(8,128)S(1)}, f32[1,128,2]{1,2,0:T(2,128)S(1)}, f32[1,128,2]{1,2,0:T(2,128)S(1)})) conditional(s32[]{:T(128)} %bitcast.112, (f32[1,128,2,128]{1,3,2,0:T(8,128)S(1)}, f32[1,128,2]{1,2,0:T(2,128)S(1)}, f32[1,128,2]{1,2,0:T(2,128)S(1)}) %tuple.96, (pred[1]{0:T(512)(128)(4,1)}, s32[]{:T(128)}, ...), branch_computations={%region_3.3_spmd, %region_4.6_spmd.clone} | conditional | flops 68782224 | bytes 2977504 | solution.py:107
  152.8 1.2 fusion.120
  154.1 1.3 fusion.10
  174.2 4.7 %conditional.3 = ((f32[1,128,2,128]{1,3,2,0:T(8,128)S(1)}, f32[1,128,2]{1,2,0:T(2,128)S(1)}, f32[1,128,2]{1,2,0:T(2,128)S(1)})) conditional(s32[]{:T(128)} %bitcast.112, (f32[1,128,2,128]{1,3,2,0:T(8,128)S(1)}, f32[1,128,2]{1,2,0:T(2,128)S(1)}, f32[1,128,2]{1,2,0:T(2,128)S(1)}) %tuple.96, (pred[1]{0:T(512)(128)(4,1)}, s32[]{:T(128)}, ...), branch_computations={%region_3.3_spmd, %region_4.6_spmd.clone} | conditional | flops 68782224 | bytes 2977504 | solution.py:107
  176.3 1.2 fusion.120
  177.7 1.3 fusion.10
  190.2 4.7 %conditional.3 = ((f32[1,128,2,128]{1,3,2,0:T(8,128)S(1)}, f32[1,128,2]{1,2,0:T(2,128)S(1)}, f32[1,128,2]{1,2,0:T(2,128)S(1)})) conditional(s32[]{:T(128)} %bitcast.112, (f32[1,128,2,128]{1,3,2,0:T(8,128)S(1)}, f32[1,128,2]{1,2,0:T(2,128)S(1)}, f32[1,128,2]{1,2,0:T(2,128)S(1)}) %tuple.96, (pred[1]{0:T(512)(128)(4,1)}, s32[]{:T(128)}, ...), branch_computations={%region_3.3_spmd, %region_4.6_spmd.clone} | conditional | flops 68782224 | bytes 2977504 | solution.py:107
  192.3 1.2 fusion.120
  193.6 1.3 fusion.10
  217.5 4.7 %conditional.3 = ((f32[1,128,2,128]{1,3,2,0:T(8,128)S(1)}, f32[1,128,2]{1,2,0:T(2,128)S(1)}, f32[1,128,2]{1,2,0:T(2,128)S(1)})) conditional(s32[]{:T(128)} %bitcast.112, (f32[1,128,2,128]{1,3,2,0:T(8,128)S(1)}, f32[1,128,2]{1,2,0:T(2,128)S(1)}, f32[1,128,2]{1,2,0:T(2,128)S(1)}) %tuple.96, (pred[1]{0:T(512)(128)(4,1)}, s32[]{:T(128)}, ...), branch_computations={%region_3.3_spmd, %region_4.6_spmd.clone} | conditional | flops 68782224 | bytes 2977504 | solution.py:107
  219.5 1.2 fusion.120
  220.9 1.3 fusion.10
  224.3 101.4 %all-gather.6.cloned.1.call-done = bf16[2048,4096]{1,0:T(8,128)(2,1)} async-done(((bf16[128,4096]{1,0:T(8,128)(2,1)}), bf16[2048,4096]{1,0:T(8,128)(2,1)}) %all-gather.6.cloned.1.call-update) | async-done | bytes 16777232 | tf_op jit(solution)/shard_map/all_gather | solution.py:122
  325.7 8.9 %reduce_sum.54 = bf16[128,4096]{1,0:T(8,128)(2,1)S(1)} reduce(bf16[16,128,4096]{2,1,0:T(8,128)(2,1)} %bitcast.113, bf16[]{:T(256)} %constant.205.clone.1), dimensions={0}, to_apply=%region_8.9 | reduce | flops 7864320 | bytes 17825794 | tf_op jit(solution)/shard_map/reduce_sum | solution.py:122
  335.3 6.4 %convolution_convert_fusion = bf16[128,4096]{1,0:T(8,128)(2,1)} fusion(bf16[512,4096]{1,0:T(8,128)(2,1)} %param.22, bf16[4096,512]{1,0:T(8,128)(2,1)} %param.21, bf16[128,4096]{1,0:T(8,128)(2,1)S(1)} %reduce_sum.54, f32[4096]{0:T(1024)S(1)} %copy-done.2, f32[128]{0:T(128)S(1)} %add_rsqrt_fusion, f32[128]{0:T(128)S(1)} %broadcast_multiply_fusion), kind=kOutput, calls=%fused_computation.40 | convolution fusion | flops 1081147392 | bytes 10503168 | tf_op jit(solution)/shard_map/dot_general | solution.py:132
  342.5 1.6 convert_element_type.83
  344.1 63.6 %reduce-scatter.2.cloned.1.call-done = bf16[128,256]{1,0:T(8,128)(2,1)} async-done(((bf16[128,4096]{1,0:T(8,128)(2,1)}), bf16[128,256]{1,0:T(8,128)(2,1)}) %reduce-scatter.2.cloned.1.call-update) | async-done | bytes 65552 | tf_op jit(solution)/shard_map/reduce_scatter | solution.py:133
  407.7 1.7 select_convert_fusion
  (145 shorter events, 19.8 us)
Async XLA Ops:
  7.2 215.1 %copy-start = (bf16[256,4096]{1,0:T(8,128)(2,1)S(1)}, bf16[256,4096]{1,0:T(8,128)(2,1)}, u32[]{:S(2)}) copy-start(bf16[256,4096]{1,0:T(8,128)(2,1)} %param.20) | copy-start | bytes 6291460
  7.2 114.7 %all-gather.4.cloned.1.call-start = ((), (), s32[]{:S(2)}) async-start(), calls=%async_computation.1 | async-start | bytes 8912896 | tf_op jit(solution)/shard_map/all_gather | solution.py:85
  7.9 317.8 %all-gather.6.cloned.1.call-start = ((), (), s32[]{:S(2)}) async-start(), calls=%async_computation.3 | async-start | bytes 17825792 | tf_op jit(solution)/shard_map/all_gather | solution.py:122
  134.4 8.8 %copy-start.3 = (s32[16]{0:T(128)S(1)}, s32[16]{0:T(128)}, u32[]{:S(2)}) copy-start(s32[16]{0:T(128)} %param.25) | copy-start | bytes 196
  222.2 0.8 copy-start.1
  224.3 183.5 %reduce-scatter.2.cloned.1.call-start = ((), (), s32[]{:S(2)}) async-start(), calls=%async_computation.2 | async-start | bytes 1114112 | tf_op jit(solution)/shard_map/reduce_scatter | solution.py:133
  334.6 0.7 copy-start.2
Sparse Core Ops, SparseCore 0:
  10.4 111.4 all-gather.3
  224.4 101.2 all-gather.5
  341.9 65.7 reduce-scatter.1
